TPU v7x, 32 devices: a whole 2x2x4 slice. The times are simulated.
32 devices in a mesh: seq: 8 (over z, x), head: 4 (over y, core).
Axes of the slice: x: 2, y: 2, z: 4, core: 2. Of those that a mesh axis runs over, the one named last changes fastest.
Arguments:
- h_in: float32 [2048, 1024], P('seq', 'head'), may hold values from -6 to 6
- norm_gain: float32 [2, 1024], P(None, 'head'), may hold values from 0.5 to 1.5
- w_z: bfloat16 [2, 1024, 2048], P(None, None, 'head'), may hold values from -0.1875 to 0.1875
- w_x: bfloat16 [2, 1024, 2048], P(None, None, 'head'), may hold values from -0.1875 to 0.1875
- w_bc: bfloat16 [2, 1024, 256], replicated, may hold values from -0.1875 to 0.1875
- w_dt: bfloat16 [2, 1024, 32], P(None, None, 'head'), may hold values from -0.1875 to 0.1875
- conv_x_w: float32 [2, 4, 2048], P(None, None, 'head'), may hold values from -3 to 3
- conv_x_b: float32 [2, 2048], P(None, 'head'), may hold values from -0.5 to 0.5
- conv_bc_w: float32 [2, 4, 256], replicated, may hold values from -3 to 3
- conv_bc_b: float32 [2, 256], replicated, may hold values from -0.5 to 0.5
- dt_bias: float32 [2, 32], P(None, 'head'), may hold values from -4 to -1
- a_log: float32 [2, 32], P(None, 'head'), may hold values from -10 to -1
- skip: float32 [2, 32], P(None, 'head'), may hold values from 0.5 to 1.5
- gate_gain: float32 [2, 2048], P(None, 'head'), may hold values from 0.5 to 1.5
- w_out: bfloat16 [2, 2048, 1024], P(None, 'head'), may hold values from -0.125 to 0.125
- d_out: float32 [2048, 1024], P('seq', 'head'), may hold values from -6 to 6
Outputs:
- h_out: float32 [2048, 1024], P('seq', 'head')
- d_h: float32 [2048, 1024], P('seq', 'head')
- d_norm_gain: float32 [2, 1024], P(None, 'head')
- d_w_z: float32 [2, 1024, 2048], P(None, 'seq', 'head')
- d_w_x: float32 [2, 1024, 2048], P(None, 'seq', 'head')
- d_w_bc: float32 [2, 1024, 256], replicated
- d_w_dt: float32 [2, 1024, 32], P(None, 'seq', 'head')
- d_conv_x_w: float32 [2, 4, 2048], P(None, None, 'head')
- d_conv_x_b: float32 [2, 2048], P(None, 'head')
- d_conv_bc_w: float32 [2, 4, 256], replicated
- d_conv_bc_b: float32 [2, 256], replicated
- d_dt_bias: float32 [2, 32], P(None, 'head')
- d_a_log: float32 [2, 32], P(None, 'head')
- d_skip: float32 [2, 32], P(None, 'head')
- d_gate_gain: float32 [2, 2048], P(None, 'head')
- d_w_out: float32 [2, 2048, 1024], P(None, 'head', 'seq')
All inputs are finite; a program needn't handle non-finite values.
Results may differ from a plain program's by a relative error of at most 0.014.
The roundings to bfloat16 on the way count: a program that leaves them out, or rounds other values in their place, can miss the bound.
Values may be sent and summed in bfloat16 or wider, within the bound.
A program may use at most 128 MiB of HBM per device.

v0:
```python
import jax
import jax.numpy as jnp
from jax import lax
from jax.sharding import PartitionSpec as P

D = 1024
HEAD_DIM = 64
STATE = 128
CONV = 4
SPAN = 256
LAYERS = 2
DI = 2048


epsilon = 1e-05
highest = lax.Precision.HIGHEST


def shifted(value, axis, steps):
    count = lax.axis_size(axis)
    first, last = (max(0, -steps), min(count, count - steps))
    return lax.ppermute(value, axis, [(source, source + steps) for source in range(first, last)])


def entering_2(value, axis, join, neutral, backward):
    count, mine = (lax.axis_size(axis), lax.axis_index(axis))
    pieces = jax.tree.map(lambda part: lax.all_gather(part, axis), value)
    if backward:
        pieces = jax.tree.map(lambda part: part[::-1], pieces)
        mine = count - 1 - mine
    total = jax.tree.map(
        lambda part, zero: jnp.full_like(part, 0) + jnp.asarray(zero, part.dtype), value, neutral
    )

    def lap(position, total):
        longer = join(total, jax.tree.map(lambda part: part[position], pieces))
        return jax.tree.map(lambda new, old: jnp.where(position < mine, new, old), longer, total)

    return lax.fori_loop(0, count - 1, lap, total)


def conv_inputs(extended, dt_raw, conv_weight, conv_bias, dt_bias, a_log):
    row_count = dt_raw.shape[0]
    mixed = jnp.zeros((row_count, extended.shape[1]), jnp.float32) + conv_bias[None, :]
    for offset in range(CONV):
        mixed = mixed + conv_weight[offset][None, :] * extended[offset : offset + row_count]
    active = jax.nn.silu(mixed)
    inner = extended.shape[1] - 2 * STATE
    head_count = dt_raw.shape[1]
    values = active[:, :inner].reshape(row_count, head_count, HEAD_DIM)
    b_proj = active[:, inner : inner + STATE]
    c_proj = active[:, inner + STATE :]
    steps_dt = jax.nn.softplus(dt_raw + dt_bias[None, :])
    log_decay = -steps_dt * jnp.exp(a_log)[None, :]
    return (values, b_proj, c_proj, steps_dt, log_decay)


def scan_from_zero(values, b_proj, c_proj, steps_dt, log_decay):
    row_count, head_count = steps_dt.shape
    blocks = row_count // SPAN
    causal = (jnp.arange(SPAN)[:, None] >= jnp.arange(SPAN)[None, :])[None]

    def one_block(carried, block_data):
        block_vals, b_blk, c_blk, dt_blk, la_blk = block_data
        cumulative = jnp.cumsum(la_blk, axis=0)
        cum_heads = cumulative.T
        spread = cum_heads[:, :, None] - cum_heads[:, None, :]
        weights = jnp.where(causal, jnp.exp(jnp.where(causal, spread, 0.0)), 0.0)
        scores = jnp.dot(c_blk, b_blk.T, precision=highest)
        scaled = block_vals * dt_blk[:, :, None]
        y_diag = jnp.einsum("htu,uhp->thp", weights * scores[None], scaled, precision=highest)
        y_off = (
            jnp.einsum("tn,hpn->thp", c_blk, carried, precision=highest)
            * jnp.exp(cumulative)[:, :, None]
        )
        ending = cumulative[-1]
        tail_decay = jnp.exp(ending[None, :] - cumulative)
        updated = carried * jnp.exp(ending)[:, None, None] + jnp.einsum(
            "uhp,un->hpn", scaled * tail_decay[:, :, None], b_blk, precision=highest
        )
        return (updated, y_diag + y_off)

    stacked = (
        values.reshape(blocks, SPAN, head_count, HEAD_DIM),
        b_proj.reshape(blocks, SPAN, STATE),
        c_proj.reshape(blocks, SPAN, STATE),
        steps_dt.reshape(blocks, SPAN, head_count),
        log_decay.reshape(blocks, SPAN, head_count),
    )
    initial = jnp.zeros((head_count, HEAD_DIM, STATE), jnp.float32)
    last_state, outputs = lax.scan(one_block, initial, stacked)
    return (outputs.reshape(row_count, head_count, HEAD_DIM), last_state)


def carry_term(c_proj, log_decay, entering):
    cumulative = jnp.cumsum(log_decay, axis=0)
    return (
        jnp.einsum("tn,hpn->thp", c_proj, entering, precision=highest)
        * jnp.exp(cumulative)[:, :, None]
    )


def link_states(earlier, later):
    return (earlier[0] * later[0], later[0][:, None, None] * earlier[1] + later[1])


def token_sums(partial_sums):
    return lax.psum(partial_sums, "head")


def contract_first(left, right):
    return lax.dot_general(
        left, right, (((0,), (0,)), ((), ())), preferred_element_type=jnp.float32
    )


def local(
    h_in,
    norm_gain,
    w_z,
    w_x,
    w_bc,
    w_dt,
    conv_x_w,
    conv_x_b,
    conv_bc_w,
    conv_bc_b,
    dt_bias,
    a_log,
    skip,
    gate_gain,
    w_out,
    d_out,
):
    row_count = h_in.shape[0]
    inner = w_x.shape[2]
    head_count = w_dt.shape[2]
    hidden = h_in
    kept = []
    for layer_idx in range(LAYERS):
        gain_one = norm_gain[layer_idx]
        full_hidden, full_gain = (
            lax.all_gather(hidden, "head", axis=1, tiled=True),
            lax.all_gather(gain_one, "head", axis=0, tiled=True),
        )
        factor = lax.rsqrt(jnp.mean(full_hidden * full_hidden, axis=1) + epsilon)
        normed = (full_hidden * factor[:, None] * full_gain[None, :]).astype(jnp.bfloat16)
        gate_in = jnp.dot(normed, w_z[layer_idx], preferred_element_type=jnp.float32)
        x_in = jnp.dot(normed, w_x[layer_idx], preferred_element_type=jnp.float32)
        bc_in = jnp.dot(normed, w_bc[layer_idx], preferred_element_type=jnp.float32)
        dt_raw = jnp.dot(normed, w_dt[layer_idx], preferred_element_type=jnp.float32)
        conv_in = jnp.concatenate([x_in, bc_in], axis=1)
        before = shifted(conv_in[row_count - (CONV - 1) :], "seq", 1)
        extended = jnp.concatenate([before, conv_in], axis=0)
        conv_weight = jnp.concatenate([conv_x_w[layer_idx], conv_bc_w[layer_idx]], axis=1)
        conv_bias = jnp.concatenate([conv_x_b[layer_idx], conv_bc_b[layer_idx]], axis=0)
        inputs, input_back = jax.vjp(
            conv_inputs,
            extended,
            dt_raw,
            conv_weight,
            conv_bias,
            dt_bias[layer_idx],
            a_log[layer_idx],
        )
        values, b_proj, c_proj, steps_dt, log_decay = inputs
        local_part, block_back = jax.vjp(
            scan_from_zero, values, b_proj, c_proj, steps_dt, log_decay
        )
        scanned, leaving = local_part
        decays = jnp.exp(jnp.sum(log_decay, axis=0))
        identity = (jnp.ones_like(decays), jnp.zeros_like(leaving))
        entering = entering_2((decays, leaving), "seq", link_states, identity, False)[1]
        carried_part, carry_back = jax.vjp(carry_term, c_proj, log_decay, entering)
        mixed = scanned + carried_part + skip[layer_idx][None, :, None] * values
        gate_act = jax.nn.silu(gate_in)
        gated = mixed.reshape(row_count, inner) * gate_act
        gate_factor = lax.rsqrt(token_sums(jnp.sum(gated * gated, axis=1)) / DI + epsilon)
        scaled = (gated * gate_factor[:, None] * gate_gain[layer_idx][None, :]).astype(jnp.bfloat16)
        out_weight = w_out[layer_idx]
        summed = lax.psum_scatter(
            contract_first(out_weight, scaled.T), "head", scatter_dimension=0, tiled=True
        )
        kept.append(
            (
                hidden,
                factor,
                normed,
                gate_in,
                gate_act,
                gated,
                gate_factor,
                scaled,
                mixed,
                values,
                decays,
                entering,
                input_back,
                block_back,
                carry_back,
            )
        )
        hidden = hidden + summed.T
    grad = d_out
    collected = [None] * LAYERS
    for layer_idx in reversed(range(LAYERS)):
        (
            layer_input,
            factor,
            normed,
            gate_in,
            gate_act,
            gated,
            gate_factor,
            scaled,
            mixed,
            values,
            decays,
            entering,
            input_back,
            block_back,
            carry_back,
        ) = kept[layer_idx]
        grad_b = grad.astype(jnp.bfloat16)
        out_weight = w_out[layer_idx]
        grad_cols = lax.all_gather(grad_b, "head", axis=1, tiled=True)
        d_part = lax.dot_general(
            grad_cols, out_weight, (((1,), (1,)), ((), ())), preferred_element_type=jnp.float32
        )
        d_cols = contract_first(scaled, grad_cols)
        normalized = gated * gate_factor[:, None]
        d_ggain = jnp.sum(d_part * normalized, axis=0)
        d_norm_in = d_part * gate_gain[layer_idx][None, :]
        along = token_sums(jnp.sum(d_norm_in * normalized, axis=1)) / DI
        d_gated = gate_factor[:, None] * (d_norm_in - normalized * along[:, None])
        sigma = jax.nn.sigmoid(gate_in)
        d_gate = d_gated * mixed.reshape(row_count, inner) * sigma * (1.0 + gate_in * (1.0 - sigma))
        d_mixed = (d_gated * gate_act).reshape(row_count, head_count, HEAD_DIM)
        d_skipped = jnp.sum(d_mixed * values, axis=(0, 2))
        d_c_carry, d_la_carry, d_entering = carry_back(d_mixed)
        back_identity = (jnp.ones_like(decays), jnp.zeros_like(d_entering))
        leaving_grad = entering_2((decays, d_entering), "seq", link_states, back_identity, True)[1]
        d_decays = jnp.sum(leaving_grad * entering, axis=(1, 2)) * decays
        d_values, d_b_proj, d_c_local, d_steps, d_la_local = block_back((d_mixed, leaving_grad))
        d_values = d_values + skip[layer_idx][None, :, None] * d_mixed
        d_inputs = (
            d_values,
            d_b_proj,
            d_c_carry + d_c_local,
            d_steps,
            d_la_carry + d_la_local + d_decays[None, :],
        )
        d_extended, d_dtraw, d_cweight, d_cbias, d_dtbias, d_alog = input_back(d_inputs)
        returned = shifted(d_extended[: CONV - 1], "seq", -1)
        d_conv = d_extended[CONV - 1 :] + jnp.pad(returned, ((row_count - (CONV - 1), 0), (0, 0)))
        d_gate_b = d_gate.astype(jnp.bfloat16)
        d_x_b = d_conv[:, :inner].astype(jnp.bfloat16)
        d_shared = d_conv[:, inner:]
        d_dt_b = d_dtraw.astype(jnp.bfloat16)
        d_wz = contract_first(normed, d_gate_b)
        d_wx = contract_first(normed, d_x_b)
        d_wdt = contract_first(normed, d_dt_b)
        d_wbc = lax.dot_general(
            normed.astype(jnp.float32), d_shared, (((0,), (0,)), ((), ())), precision=highest
        )
        wz_now = w_z[layer_idx]
        wx_now = w_x[layer_idx]
        wdt_now = w_dt[layer_idx]
        wbc_now = w_bc[layer_idx]

        def product(weight, grads):
            return lax.dot_general(
                weight, grads, (((1,), (1,)), ((), ())), preferred_element_type=jnp.float32
            )

        shared_rows = wbc_now.astype(jnp.float32)
        shared_term = lax.dot_general(
            shared_rows, d_shared, (((1,), (1,)), ((), ())), precision=highest
        )
        d_normed = lax.psum_scatter(
            product(wz_now, d_gate_b)
            + product(wx_now, d_x_b)
            + product(wdt_now, d_dt_b)
            + shared_term,
            "head",
            scatter_dimension=0,
            tiled=True,
        ).T
        centered = layer_input * factor[:, None]
        d_ngain = jnp.sum(d_normed * centered, axis=0)
        d_unit = d_normed * norm_gain[layer_idx][None, :]
        along_in = token_sums(jnp.sum(d_unit * centered, axis=1)) / D
        grad = grad + factor[:, None] * (d_unit - centered * along_in[:, None])
        collected[layer_idx] = (
            d_wz,
            d_wx,
            d_wdt,
            d_cols,
            d_ngain,
            d_cweight[:, :inner],
            d_cbias[:inner],
            d_ggain,
            d_dtbias,
            d_alog,
            d_skipped,
            d_wbc,
            d_cweight[:, inner:],
            d_cbias[inner:],
        )
    stacks = [
        jnp.stack([collected[layer_idx][member] for layer_idx in range(LAYERS)])
        for member in range(14)
    ]
    weight_sums = (
        lax.psum_scatter(
            stacks[0].astype(jnp.bfloat16), "seq", scatter_dimension=1, tiled=True
        ).astype(jnp.float32),
        lax.psum_scatter(
            stacks[1].astype(jnp.bfloat16), "seq", scatter_dimension=1, tiled=True
        ).astype(jnp.float32),
        lax.psum_scatter(
            stacks[2].astype(jnp.bfloat16), "seq", scatter_dimension=1, tiled=True
        ).astype(jnp.float32),
        lax.psum_scatter(
            stacks[3].astype(jnp.bfloat16), "seq", scatter_dimension=2, tiled=True
        ).astype(jnp.float32),
    )
    vector_sums = lax.psum(
        (stacks[4], stacks[5], stacks[6], stacks[7], stacks[8], stacks[9], stacks[10]), "seq"
    )
    shared_sums = lax.psum((stacks[11], stacks[12], stacks[13]), ("seq", "head"))
    return (
        hidden,
        grad,
        vector_sums[0],
        weight_sums[0],
        weight_sums[1],
        shared_sums[0],
        weight_sums[2],
        vector_sums[1],
        vector_sums[2],
        shared_sums[1],
        shared_sums[2],
        vector_sums[4],
        vector_sums[5],
        vector_sums[6],
        vector_sums[3],
        weight_sums[3],
    )


def solution(mesh):
    return jax.shard_map(
        local,
        mesh=mesh,
        in_specs=(
            P("seq", "head"),
            P(None, "head"),
            P(None, None, "head"),
            P(None, None, "head"),
            P(),
            P(None, None, "head"),
            P(None, None, "head"),
            P(None, "head"),
            P(),
            P(),
            P(None, "head"),
            P(None, "head"),
            P(None, "head"),
            P(None, "head"),
            P(None, "head", None),
            P("seq", "head"),
        ),
        out_specs=(
            P("seq", "head"),
            P("seq", "head"),
            P(None, "head"),
            P(None, "seq", "head"),
            P(None, "seq", "head"),
            P(),
            P(None, "seq", "head"),
            P(None, None, "head"),
            P(None, "head"),
            P(),
            P(),
            P(None, "head"),
            P(None, "head"),
            P(None, "head"),
            P(None, "head"),
            P(None, "head", "seq"),
        ),
        check_vma=False,
    )
```

profile of v0, /device:TPU:0, one launch (start us, length us, event | category | flops | bytes accessed | tf_op | source)
XLA Modules:
  0.0 995.1 jit_solution(10929443034664853142)
XLA Ops:
  8.7 6.0 all-gather
  22.1 6.9 all-gather.15.cloned.1.call-done
  32.9 3.4 collective-permute-start
  45.5 21.2 %all-reduce.26 = f32[64]{0:T(128)S(1)} all-reduce(f32[64]{0:T(128)S(1)} %exponential_dynamic-update-slice_fusion.1), channel_id=3, replica_groups=mesh['seq'=8,'head'=4] {'seq'}, use_global_device_ids=true, to_apply=%add.26 | all-reduce | flops 64 | bytes 512
  68.5 23.3 %all-gather.19.cloned.1.call-done = f32[64,64,128]{2,1,0:T(8,128)} async-done(((f32[8,64,128]{2,1,0:T(8,128)}), f32[64,64,128]{2,1,0:T(8,128)}) %all-gather.19.cloned.1.call-update) | async-done | bytes 2097168 | tf_op jit(solution)/shard_map/all_gather | solution.py:27
  91.8 7.6 while.44
  100.1 4.4 fusion.58
  109.1 5.8 psum.112
  115.0 2.7 convolution_bitcast_fusion.3
  117.8 23.7 %reduce-scatter.13.cloned.1.call-done = f32[256,256]{0,1:T(8,128)} async-done(((f32[1024,256]{0,1:T(8,128)}), f32[256,256]{0,1:T(8,128)}) %reduce-scatter.13.cloned.1.call-update) | async-done | bytes 262160 | tf_op jit(solution)/shard_map/reduce_scatter | solution.py:181
  143.2 5.1 all-gather.3
  149.6 10.6 %all-gather.17.cloned.1.call-done = f32[256,1024]{1,0:T(8,128)} async-done(((f32[256,256]{1,0:T(8,128)}), f32[256,1024]{1,0:T(8,128)}) %all-gather.17.cloned.1.call-update) | async-done | bytes 1048592 | tf_op jit(solution)/shard_map/all_gather | solution.py:143
  167.1 3.4 collective-permute-start.1
  181.6 7.0 all_gather.64
  189.3 22.7 %all-reduce.27 = f32[64]{0:T(128)S(1)} all-reduce(f32[64]{0:T(128)S(1)} %exponential_dynamic-update-slice_fusion), channel_id=6, replica_groups=mesh['seq'=8,'head'=4] {'seq'}, use_global_device_ids=true, to_apply=%add.27 | all-reduce | flops 64 | bytes 512
  217.7 13.2 %all-gather.21.cloned.1.call-done = f32[64,64,128]{2,1,0:T(8,128)} async-done(((f32[8,64,128]{2,1,0:T(8,128)}), f32[64,64,128]{2,1,0:T(8,128)}) %all-gather.21.cloned.1.call-update) | async-done | bytes 2097168 | tf_op jit(solution)/shard_map/all_gather | solution.py:27
  230.9 15.9 %while.45 = (s32[]{:T(128)}, f32[8,64,128]{2,1,0:T(8,128)S(1)}, s32[]{:T(128)}, f32[8,8]{1,0:T(8,128)}, f32[8,8,64,128]{3,2,1,0:T(8,128)}, /*index=5*/s32[]{:T(128)}, s32[]{:T(128)}) while((s32[]{:T(128)}, f32[8,64,128]{2,1,0:T(8,128)S(1)}, s32[]{:T(128)}, f32[8,8]{1,0:T(8,128)}, f32[8,8,64,128]{3,2,1,0:T(8,128)}, ...), condition=%wide.region_14.16_spmd.clone, body=%wide.region_13.15_spmd.clone.sunk | while | flops 262148 | bytes 786633 | solution.py:39
  248.3 4.9 fusion.61
  255.3 2.8 multiply_reduce_fusion.26
  258.1 5.6 psum.113
  263.7 3.4 multiply_reduce_fusion.12
  267.1 6.6 psum.114
  273.7 3.5 multiply_reduce_fusion.14
  290.6 3.2 reduce-window.88
  297.0 2.7 convolution_bitcast_fusion.9
  299.7 2.8 fusion.71
  302.5 3.9 fusion.37
  306.4 22.6 %all-gather.23.cloned.1.call-done = f32[64,64,128]{2,1,0:T(8,128)} async-done(((f32[8,64,128]{2,1,0:T(8,128)}), f32[64,64,128]{2,1,0:T(8,128)}) %all-gather.23.cloned.1.call-update) | async-done | bytes 2097168 | tf_op jit(solution)/shard_map/all_gather | solution.py:27
  329.0 3.2 rev.13
  332.1 15.8 %while.46 = (s32[]{:T(128)}, f32[8,64,128]{2,1,0:T(8,128)S(1)}, s32[]{:T(128)}, f32[8,8]{1,0:T(8,128)}, f32[8,8,64,128]{3,2,1,0:T(8,128)}, /*index=5*/s32[]{:T(128)}, s32[]{:T(128)}) while((s32[]{:T(128)}, f32[8,64,128]{2,1,0:T(8,128)S(1)}, s32[]{:T(128)}, f32[8,8]{1,0:T(8,128)}, f32[8,8,64,128]{3,2,1,0:T(8,128)}, ...), condition=%wide.region_22.24_spmd.clone, body=%wide.region_21.23_spmd.clone.sunk | while | flops 262148 | bytes 786633 | solution.py:39
  350.3 2.7 convolution_bitcast_fusion.7
  353.0 3.4 multiply_reduce_fusion.22
  358.9 2.7 reduce-window.90
  379.2 3.2 collective-permute-done.2
  385.8 2.7 convolution_bitcast_fusion.2
  388.6 21.4 %reduce-scatter.17.cloned.1.call-done = f32[256,256]{0,1:T(8,128)} async-done(((f32[1024,256]{0,1:T(8,128)}), f32[256,256]{0,1:T(8,128)}) %reduce-scatter.17.cloned.1.call-update) | async-done | bytes 262160 | tf_op jit(solution)/shard_map/reduce_scatter | solution.py:280
  411.7 5.7 psum.115
  417.5 19.9 %reduce-scatter.15.cloned.1.call-done = f32[256,256]{0,1:T(8,128)} async-done(((f32[1024,256]{0,1:T(8,128)}), f32[256,256]{0,1:T(8,128)}) %reduce-scatter.15.cloned.1.call-update) | async-done | bytes 262160 | tf_op jit(solution)/shard_map/reduce_scatter | solution.py:181
  439.6 6.7 all_gather.67
  449.0 6.7 psum.116
  455.6 3.2 multiply_reduce_fusion.15
  462.1 2.9 fusion.21
  465.3 2.7 reduce-window.92
  468.7 2.8 fusion.20
  471.5 3.9 fusion.39
  475.4 35.6 %all-gather.25.cloned.1.call-done = f32[64,64,128]{2,1,0:T(8,128)} async-done(((f32[8,64,128]{2,1,0:T(8,128)}), f32[64,64,128]{2,1,0:T(8,128)}) %all-gather.25.cloned.1.call-update) | async-done | bytes 2097168 | tf_op jit(solution)/shard_map/all_gather | solution.py:27
  511.0 3.2 rev.15
  514.2 12.3 %while.47 = (s32[]{:T(128)}, f32[8,64,128]{2,1,0:T(8,128)S(1)}, s32[]{:T(128)}, f32[8,8]{1,0:T(8,128)}, f32[8,8,64,128]{3,2,1,0:T(8,128)}, /*index=5*/s32[]{:T(128)}, s32[]{:T(128)}) while((s32[]{:T(128)}, f32[8,64,128]{2,1,0:T(8,128)S(1)}, s32[]{:T(128)}, f32[8,8]{1,0:T(8,128)}, f32[8,8,64,128]{3,2,1,0:T(8,128)}, ...), condition=%wide.region_43.45_spmd.clone, body=%wide.region_42.44_spmd.clone.sunk | while | flops 262148 | bytes 786633 | solution.py:39
  527.8 4.6 multiply_reduce_fusion.17
  543.1 3.1 pad_maximum_fusion.3
  546.2 6.2 copy.152
  552.3 3.5 copy.154
  563.9 2.7 convolution_bitcast_fusion.6
  566.6 2.7 fusion.81
  585.0 4.0 collective-permute-done.3
  597.7 41.8 %all-reduce.28 = (f32[2,4,256]{2,1,0:T(4,128)}, f32[2,256]{1,0:T(2,128)}) all-reduce(f32[2,4,256]{2,1,0:T(4,128)S(1)} %pad_maximum_fusion.8, f32[2,256]{1,0:T(2,128)S(1)} %pad_maximum_fusion.16), channel_id=1, replica_groups=mesh['seq'=8,'head'=4] {'seq','head'}, use_global_device_ids=true, to_apply=%region_79.81 | all-reduce | flops 2560 | bytes 20480 | tf_op jit(solution)/shard_map/psum | solution.py:331
  643.6 31.7 %reduce-scatter.27.cloned.1.call-done = bf16[128,1024]{1,0:T(8,128)(2,1)} async-done(((bf16[1024,1024]{1,0:T(8,128)(2,1)}), bf16[128,1024]{1,0:T(8,128)(2,1)}) %reduce-scatter.27.cloned.1.call-update) | async-done | bytes 262160
  677.5 69.4 %reduce-scatter.21.cloned.1.call-done = bf16[2,128,512]{2,1,0:T(8,128)(2,1)} async-done(((bf16[2,1024,512]{2,1,0:T(8,128)(2,1)}), bf16[2,128,512]{2,1,0:T(8,128)(2,1)}) %reduce-scatter.21.cloned.1.call-update) | async-done | bytes 262160 | tf_op jit(solution)/shard_map/reduce_scatter | solution.py:315
  748.7 24.5 %reduce-scatter.19.cloned.1.call-done = f32[256,256]{0,1:T(8,128)} async-done(((f32[1024,256]{0,1:T(8,128)}), f32[256,256]{0,1:T(8,128)}) %reduce-scatter.19.cloned.1.call-update) | async-done | bytes 262160 | tf_op jit(solution)/shard_map/reduce_scatter | solution.py:280
  774.4 5.8 psum.117
  780.1 38.2 %all-reduce.29 = (f32[2,256]{1,0:T(2,128)}, f32[2,4,512]{2,1,0:T(4,128)}, f32[2,512]{1,0:T(2,128)}, f32[2,8]{1,0:T(2,128)}, f32[2,8]{1,0:T(2,128)}, /*index=5*/f32[2,8]{1,0:T(2,128)}, f32[2,512]{1,0:T(2,128)}) all-reduce(f32[2,256]{1,0:T(2,128)S(1)} %pad_maximum_fusion.15, ...), channel_id=1, replica_groups=mesh['seq'=8,'head'=4] {'seq'}, use_global_device_ids=true, to_apply=%region_62.64 | all-reduce | flops 6704 | bytes 53632 | tf_op jit(solution)/shard_map/psum | solution.py:328
  820.2 25.9 %reduce-scatter.23.cloned.1.call-done = bf16[2,128,512]{2,1,0:T(8,128)(2,1)} async-done(((bf16[2,1024,512]{2,1,0:T(8,128)(2,1)}), bf16[2,128,512]{2,1,0:T(8,128)(2,1)}) %reduce-scatter.23.cloned.1.call-update) | async-done | bytes 262160 | tf_op jit(solution)/shard_map/reduce_scatter | solution.py:318
  847.9 137.2 %all-reduce.32.cloned.1.call-done = f32[2,1024,256]{2,1,0:T(8,128)} async-done(((f32[2,1024,256]{2,1,0:T(8,128)}), f32[2,1024,256]{2,1,0:T(8,128)}) %all-reduce.32.cloned.1.call-update) | async-done | bytes 2097168 | tf_op jit(solution)/shard_map/psum | solution.py:331
  985.0 3.0 copy.196
  (598 shorter events, 219.5 us)
Async XLA Ops:
  7.2 21.8 %all-gather.15.cloned.1.call-start = ((), (), s32[]{:S(2)}) async-start(), calls=%async_computation.8 | async-start | bytes 1310720 | tf_op jit(solution)/shard_map/all_gather | solution.py:143
  7.9 83.9 %all-gather.19.cloned.1.call-start = ((), (), s32[]{:S(2)}) async-start(), calls=%async_computation.17 | async-start | bytes 2359296 | tf_op jit(solution)/shard_map/all_gather | solution.py:27
  8.7 21.8 %copy-start.101 = (f32[1,256]{1,0:T(1,128)}, f32[1,256]{1,0:T(1,128)S(1)}, u32[]{:S(2)}) copy-start(f32[1,256]{1,0:T(1,128)S(1)} %get-tuple-element.1313) | copy-start | bytes 3076
  8.7 134.5 %copy-start.103 = (f32[1,256]{1,0:T(1,128)}, f32[1,256]{1,0:T(1,128)S(1)}, u32[]{:S(2)}) copy-start(f32[1,256]{1,0:T(1,128)S(1)} %get-tuple-element.1312) | copy-start | bytes 3076
  16.8 22.1 %copy-start.70 = (f32[768]{0:T(1024)}, f32[768]{0:T(1024)S(1)}, u32[]{:S(2)}) copy-start(f32[768]{0:T(1024)S(1)} %get-tuple-element.1200) | copy-start | bytes 9220
  16.8 22.1 %copy-start.72 = (f32[768]{0:T(1024)}, f32[768]{0:T(1024)S(1)}, u32[]{:S(2)}) copy-start(f32[768]{0:T(1024)S(1)} %get-tuple-element.1201) | copy-start | bytes 9220
  16.8 22.1 %copy-start.74 = (f32[768]{0:T(1024)}, f32[768]{0:T(1024)S(1)}, u32[]{:S(2)}) copy-start(f32[768]{0:T(1024)S(1)} %get-tuple-element.1202) | copy-start | bytes 9220
  16.8 22.1 %copy-start.76 = (f32[768]{0:T(1024)}, f32[768]{0:T(1024)S(1)}, u32[]{:S(2)}) copy-start(f32[768]{0:T(1024)S(1)} %get-tuple-element.1203) | copy-start | bytes 9220
  22.1 14.4 %copy-start.120 = (f32[8]{0:T(128)}, f32[8]{0:T(128)S(1)}, u32[]{:S(2)}) copy-start(f32[8]{0:T(128)S(1)} %get-tuple-element.1321) | copy-start | bytes 100
  32.9 6.0 collective-permute-start
  40.3 59.1 %copy-start = (f32[256,768]{1,0:T(8,128)}, f32[256,768]{1,0:T(8,128)S(1)}, u32[]{:S(2)}) copy-start(f32[256,768]{1,0:T(8,128)S(1)} %get-tuple-element.1275) | copy-start | bytes 2359300
  40.7 59.4 %copy-start.17 = (f32[256,512]{0,1:T(8,128)}, f32[256,512]{0,1:T(8,128)S(1)}, u32[]{:S(2)}) copy-start(f32[256,512]{0,1:T(8,128)S(1)} %copy.129) | copy-start | bytes 1572868
  42.3 99.1 %reduce-scatter.13.cloned.1.call-start = ((), (), s32[]{:S(2)}) async-start(), calls=%async_computation.9 | async-start | bytes 1310720 | tf_op jit(solution)/shard_map/reduce_scatter | solution.py:181
  44.8 55.2 %copy-start.134 = (f32[8]{0:T(128)}, f32[8]{0:T(128)S(1)}, u32[]{:S(2)}) copy-start(f32[8]{0:T(128)S(1)} %get-tuple-element.1317) | copy-start | bytes 100
  45.4 69.5 %copy-start.88 = (f32[1,512]{1,0:T(1,128)}, f32[1,512]{1,0:T(1,128)S(1)}, u32[]{:S(2)}) copy-start(f32[1,512]{1,0:T(1,128)S(1)} %get-tuple-element.1307) | copy-start | bytes 6148
  66.8 33.2 %copy-start.82 = (f32[8,256]{1,0:T(8,128)}, f32[8,256]{1,0:T(8,128)S(1)}, u32[]{:S(2)}) copy-start(f32[8,256]{1,0:T(8,128)S(1)} %add_bitcast_fusion.3) | copy-start | bytes 24580
  68.5 31.5 %copy-start.44 = (f32[256,8,64]{0,2,1:T(8,128)}, f32[256,8,64]{0,2,1:T(8,128)S(1)}, u32[]{:S(2)}) copy-start(f32[256,8,64]{0,2,1:T(8,128)S(1)} %fusion.196) | copy-start | bytes 1572868
  109.1 34.0 %copy-start.22 = (f32[256,512]{1,0:T(8,128)}, f32[256,512]{1,0:T(8,128)S(1)}, u32[]{:S(2)}) copy-start(f32[256,512]{1,0:T(8,128)S(1)} %get-tuple-element.1272) | copy-start | bytes 1572868
  109.1 32.3 %copy-start.28 = (f32[256,256]{1,0:T(8,128)S(1)}, f32[256,256]{1,0:T(8,128)}, u32[]{:S(2)}) copy-start(f32[256,256]{1,0:T(8,128)} %param.25) | copy-start | bytes 786436
  114.9 28.2 %copy-start.93 = (f32[256]{0:T(256)}, f32[256]{0:T(256)S(1)}, u32[]{:S(2)}) copy-start(f32[256]{0:T(256)S(1)} %add_rsqrt_fusion.2) | copy-start | bytes 3076
  114.9 33.4 %copy-start.107 = (f32[4,256]{1,0:T(4,128)S(1)}, f32[4,256]{1,0:T(4,128)}, u32[]{:S(2)}) copy-start(f32[4,256]{1,0:T(4,128)} %get-tuple-element.1303) | copy-start | bytes 12292
  114.9 34.0 %copy-start.119 = (f32[1,512]{1,0:T(1,128)S(1)}, f32[1,512]{1,0:T(1,128)}, u32[]{:S(2)}) copy-start(f32[1,512]{1,0:T(1,128)} %get-tuple-element.1308) | copy-start | bytes 6148
  115.0 34.0 %copy-start.128 = (f32[1,256]{1,0:T(1,128)S(1)}, f32[1,256]{1,0:T(1,128)}, u32[]{:S(2)}) copy-start(f32[1,256]{1,0:T(1,128)} %get-tuple-element.1310) | copy-start | bytes 3076
  117.7 42.5 %all-gather.17.cloned.1.call-start = ((), (), s32[]{:S(2)}) async-start(), calls=%async_computation.10 | async-start | bytes 1310720 | tf_op jit(solution)/shard_map/all_gather | solution.py:143
  143.2 87.7 %all-gather.21.cloned.1.call-start = ((), (), s32[]{:S(2)}) async-start(), calls=%async_computation.18 | async-start | bytes 2359296 | tf_op jit(solution)/shard_map/all_gather | solution.py:27
  167.1 4.8 collective-permute-start.1
  180.5 148.4 %all-gather.23.cloned.1.call-start = ((), (), s32[]{:S(2)}) async-start(), calls=%async_computation.19 | async-start | bytes 2359296 | tf_op jit(solution)/shard_map/all_gather | solution.py:27
  215.3 33.0 %copy-start.58 = (f32[256,256]{1,0:T(8,128)}, f32[256,256]{1,0:T(8,128)S(1)}, u32[]{:S(2)}) copy-start(f32[256,256]{1,0:T(8,128)S(1)} %fusion.205) | copy-start | bytes 786436
  230.9 17.4 %copy-start.84 = (f32[8,256]{1,0:T(8,128)S(1)}, f32[8,256]{1,0:T(8,128)}, u32[]{:S(2)}) copy-start(f32[8,256]{1,0:T(8,128)} %add_bitcast_fusion.1) | copy-start | bytes 24580
  263.7 13.5 %copy-start.95 = (f32[256]{0:T(256)}, f32[256]{0:T(256)S(1)}, u32[]{:S(2)}) copy-start(f32[256]{0:T(256)S(1)} %add_rsqrt_fusion) | copy-start | bytes 3076
  281.6 128.5 %reduce-scatter.17.cloned.1.call-start = ((), (), s32[]{:S(2)}) async-start(), calls=%async_computation.12 | async-start | bytes 1310720 | tf_op jit(solution)/shard_map/reduce_scatter | solution.py:280
  332.1 18.2 %copy-start.62 = (f32[256,8]{0,1:T(8,128)S(1)}, f32[256,8]{0,1:T(8,128)}, u32[]{:S(2)}) copy-start(f32[256,8]{0,1:T(8,128)} %subtract_exponential_fusion) | copy-start | bytes 24580
  353.0 12.5 %copy-start.25 = (f32[256,512]{1,0:T(8,128)S(1)}, f32[256,512]{1,0:T(8,128)}, u32[]{:S(2)}) copy-start(f32[256,512]{1,0:T(8,128)} %get-tuple-element.1256) | copy-start | bytes 1572868
  376.8 5.6 collective-permute-start.2
  385.7 24.4 %copy-start.30 = (f32[256,256]{1,0:T(8,128)S(1)}, f32[256,256]{1,0:T(8,128)}, u32[]{:S(2)}) copy-start(f32[256,256]{1,0:T(8,128)} %bitcast_add_fusion.5) | copy-start | bytes 786436
  385.7 24.3 %copy-start.104 = (f32[1,256]{1,0:T(1,128)S(1)}, f32[1,256]{1,0:T(1,128)}, u32[]{:S(2)}) copy-start(f32[1,256]{1,0:T(1,128)} %copy-done.103) | copy-start | bytes 3076
  385.7 24.3 %copy-start.111 = (f32[256]{0:T(256)S(1)}, f32[256]{0:T(256)}, u32[]{:S(2)}) copy-start(f32[256]{0:T(256)} %copy-done.110) | copy-start | bytes 3076
  385.7 51.7 %reduce-scatter.15.cloned.1.call-start = ((), (), s32[]{:S(2)}) async-start(), calls=%async_computation.11 | async-start | bytes 1310720 | tf_op jit(solution)/shard_map/reduce_scatter | solution.py:181
  388.5 58.5 %copy-start.23 = (f32[256,512]{1,0:T(8,128)S(1)}, f32[256,512]{1,0:T(8,128)}, u32[]{:S(2)}) copy-start(f32[256,512]{1,0:T(8,128)} %copy-done.22) | copy-start | bytes 1572868
  388.5 58.5 %copy-start.89 = (f32[1,512]{1,0:T(1,128)S(1)}, f32[1,512]{1,0:T(1,128)}, u32[]{:S(2)}) copy-start(f32[1,512]{1,0:T(1,128)} %copy-done.88) | copy-start | bytes 6148
  388.5 58.5 %copy-start.94 = (f32[256]{0:T(256)S(1)}, f32[256]{0:T(256)}, u32[]{:S(2)}) copy-start(f32[256]{0:T(256)} %copy-done.93) | copy-start | bytes 3076
  388.6 122.4 %all-gather.25.cloned.1.call-start = ((), (), s32[]{:S(2)}) async-start(), calls=%async_computation.20 | async-start | bytes 2359296 | tf_op jit(solution)/shard_map/all_gather | solution.py:27
  439.6 16.1 %copy-start.1 = (f32[256,768]{1,0:T(8,128)S(1)}, f32[256,768]{1,0:T(8,128)}, u32[]{:S(2)}) copy-start(f32[256,768]{1,0:T(8,128)} %copy-done) | copy-start | bytes 2359300
  461.4 180.5 %reduce-scatter.25.cloned.1.call-start = ((), (), s32[]{:S(2)}) async-start(), calls=%async_computation.21 | async-start | bytes 294912
  527.8 10.5 %copy-start.64 = (f32[256,8]{0,1:T(8,128)S(1)}, f32[256,8]{0,1:T(8,128)}, u32[]{:S(2)}) copy-start(f32[256,8]{0,1:T(8,128)} %copy-done.63) | copy-start | bytes 24580
  543.1 132.2 %reduce-scatter.27.cloned.1.call-start = ((), (), s32[]{:S(2)}) async-start(), calls=%async_computation.22 | async-start | bytes 2359296
  555.9 191.0 %reduce-scatter.21.cloned.1.call-start = ((), (), s32[]{:S(2)}) async-start(), calls=%async_computation.14 | async-start | bytes 2359296 | tf_op jit(solution)/shard_map/reduce_scatter | solution.py:315
  560.2 213.0 %reduce-scatter.19.cloned.1.call-start = ((), (), s32[]{:S(2)}) async-start(), calls=%async_computation.13 | async-start | bytes 1310720 | tf_op jit(solution)/shard_map/reduce_scatter | solution.py:280
  583.2 5.9 collective-permute-start.3
  592.1 254.0 %reduce-scatter.23.cloned.1.call-start = ((), (), s32[]{:S(2)}) async-start(), calls=%async_computation.15 | async-start | bytes 2359296 | tf_op jit(solution)/shard_map/reduce_scatter | solution.py:318
  594.7 44.8 %copy-start.124 = (f32[2,8]{1,0:T(2,128)S(1)}, f32[2,8]{1,0:T(2,128)}, u32[]{:S(2)}) copy-start(f32[2,8]{1,0:T(2,128)} %param.36) | copy-start | bytes 196
  594.7 44.8 %copy-start.129 = (f32[8]{0:T(128)S(1)}, f32[8]{0:T(128)}, u32[]{:S(2)}) copy-start(f32[8]{0:T(128)} %get-tuple-element.1295) | copy-start | bytes 100
  594.7 44.8 %copy-start.130 = (f32[8]{0:T(128)S(1)}, f32[8]{0:T(128)}, u32[]{:S(2)}) copy-start(f32[8]{0:T(128)} %get-tuple-element.1294) | copy-start | bytes 100
  594.7 44.8 %copy-start.132 = (f32[8]{0:T(128)S(1)}, f32[8]{0:T(128)}, u32[]{:S(2)}) copy-start(f32[8]{0:T(128)} %get-tuple-element.1259) | copy-start | bytes 100
  594.7 44.8 %copy-start.133 = (f32[8]{0:T(128)S(1)}, f32[8]{0:T(128)}, u32[]{:S(2)}) copy-start(f32[8]{0:T(128)} %get-tuple-element.1257) | copy-start | bytes 100
  594.7 44.8 %copy-start.136 = (f32[512]{0:T(512)S(1)}, f32[512]{0:T(512)}, u32[]{:S(2)}) copy-start(f32[512]{0:T(512)} %get-tuple-element.1174) | copy-start | bytes 6148
  594.8 44.8 %copy-start.137 = (f32[512]{0:T(512)S(1)}, f32[512]{0:T(512)}, u32[]{:S(2)}) copy-start(f32[512]{0:T(512)} %get-tuple-element.1172) | copy-start | bytes 6148
  594.8 390.2 %all-reduce.32.cloned.1.call-start = ((), (), s32[]{:S(2)}) async-start(), calls=%async_computation.16 | async-start | bytes 4194304 | tf_op jit(solution)/shard_map/psum | solution.py:331
  597.4 43.0 %copy-start.31 = (f32[1,1024,256]{2,1,0:T(8,128)S(1)}, f32[1,1024,256]{2,1,0:T(8,128)}, u32[]{:S(2)}) copy-start(f32[1,1024,256]{2,1,0:T(8,128)} %convolution_bitcast_fusion) | copy-start | bytes 3145732
  641.8 131.4 %copy-start.29 = (f32[256,256]{1,0:T(8,128)S(1)}, f32[256,256]{1,0:T(8,128)}, u32[]{:S(2)}) copy-start(f32[256,256]{1,0:T(8,128)} %param.25) | copy-start | bytes 786436
  641.9 131.4 %copy-start.102 = (f32[1,256]{1,0:T(1,128)S(1)}, f32[1,256]{1,0:T(1,128)}, u32[]{:S(2)}) copy-start(f32[1,256]{1,0:T(1,128)} %copy-done.101) | copy-start | bytes 3076
  641.9 131.4 %copy-start.109 = (f32[256]{0:T(256)S(1)}, f32[256]{0:T(256)}, u32[]{:S(2)}) copy-start(f32[256]{0:T(256)} %copy-done.108) | copy-start | bytes 3076
  641.9 138.2 %copy-start.123 = (f32[256]{0:T(256)S(1)}, f32[256]{0:T(256)}, u32[]{:S(2)}) copy-start(f32[256]{0:T(256)} %get-tuple-element.1182) | copy-start | bytes 3076
  641.9 176.5 %copy-start.55 = (f32[256,256]{1,0:T(8,128)S(1)}, f32[256,256]{1,0:T(8,128)}, u32[]{:S(2)}) copy-start(f32[256,256]{1,0:T(8,128)} %get-tuple-element.1264) | copy-start | bytes 786436
  (98 other events, 337.3 us)
Sparse Core Ops, SparseCore 0:
  9.5 19.4 all-gather.14
  42.4 49.3 all-gather.18
  117.8 23.5 reduce-scatter.12
  143.4 16.6 all-gather.16
  180.7 50.1 all-gather.20
  281.7 47.2 all-gather.22
  385.8 24.1 reduce-scatter.16
  412.6 24.7 reduce-scatter.14
  461.5 49.4 all-gather.24
  543.2 60.5 reduce-scatter.24
  607.4 67.9 reduce-scatter.26
  679.3 67.6 reduce-scatter.20
  749.5 23.7 reduce-scatter.18
  776.6 69.4 reduce-scatter.22
  851.3 133.7 all-reduce.31
where the time goes:
time: 1010 us; the launch traced here: 995 us
  waiting for transfers between devices  475 us (47%)
  blocking collectives  185 us (18%)
  other arithmetic  110 us (11%)
  matrix products  100 us (10%)
  local copies, waits for them, and re-layouts  96.9 us (10%)
  between operations  17.1 us (2%)
  starting transfers between devices  10.5 us (1%)
    psum x1, waiting for transfers between devices, local(): lax.psum((stacks[11], stacks[12], stacks[13]), ('seq', 'head'))  137 us
    all_gather x4, waiting for transfers between devices, entering_2(): pieces = jax.tree.map(lambda part: lax.all_gather(part, axis), value)  94.6 us
    reduce_scatter x1, waiting for transfers between devices, local(): lax.psum_scatter(stacks[0].astype(jnp.bfloat16), 'seq', scatter_dimension...  69.4 us
    reduce_scatter x2, waiting for transfers between devices, local(): lax.psum_scatter(product(wz_now, d_gate_b) + product(wx_now, d_x_b) + pro...  45.9 us
    unnamed x2, blocking collectives  43.9 us
    reduce_scatter x2, waiting for transfers between devices, local(): lax.psum_scatter(contract_first(out_weight, scaled.T), 'head', scatter_di...  43.6 us
    psum x1, blocking collectives, local(): lax.psum((stacks[11], stacks[12], stacks[13]), ('seq', 'head'))  41.8 us
    psum x1, blocking collectives, local(): lax.psum((stacks[4], stacks[5], stacks[6], stacks[7], stacks[8], stacks[9...  38.2 us
  transfers between devices with their start and end apart: 19, of which 17 were waited for; matrix products, arithmetic and copies ran while one was open for 13% of the time, Pallas kernels for 0%

commit v1 on v0

--- a/solution.py
+++ b/solution.py
@@ -22,21 +22,26 @@
     return lax.ppermute(value, axis, [(source, source + steps) for source in range(first, last)])
 
 
-def entering_2(value, axis, join, neutral, backward):
+def entering_state(log_total, value, axis, backward):
     count, mine = (lax.axis_size(axis), lax.axis_index(axis))
-    pieces = jax.tree.map(lambda part: lax.all_gather(part, axis), value)
+    heads, head_dim, state = value.shape
+    rows = jnp.broadcast_to(log_total[:, None], (heads, state))
+    packed = jnp.concatenate([value.reshape(heads * head_dim, state), rows], axis=0)
+    pieces = lax.all_gather(packed, axis)
+    values = pieces[:, : heads * head_dim].reshape(count, heads, head_dim, state)
+    logs = pieces[:, heads * head_dim :, 0]
+    source = jnp.arange(count)[:, None]
+    middle = jnp.arange(count)[None, :]
     if backward:
-        pieces = jax.tree.map(lambda part: part[::-1], pieces)
-        mine = count - 1 - mine
-    total = jax.tree.map(
-        lambda part, zero: jnp.full_like(part, 0) + jnp.asarray(zero, part.dtype), value, neutral
-    )
-
-    def lap(position, total):
-        longer = join(total, jax.tree.map(lambda part: part[position], pieces))
-        return jax.tree.map(lambda new, old: jnp.where(position < mine, new, old), longer, total)
-
-    return lax.fori_loop(0, count - 1, lap, total)
+        between, used = ((middle < source) & (middle > mine), jnp.arange(count) > mine)
+    else:
+        between, used = ((middle > source) & (middle < mine), jnp.arange(count) < mine)
+    total = jnp.sum(jnp.where(between[:, :, None], logs[None], 0.0), axis=1)
+    weights = jnp.where(used[:, None], jnp.exp(total), 0.0)
+    result = weights[0][:, None, None] * values[0]
+    for place in range(1, count):
+        result = result + weights[place][:, None, None] * values[place]
+    return result
 
 
 def conv_inputs(extended, dt_raw, conv_weight, conv_bias, dt_bias, a_log):
@@ -57,8 +62,7 @@
 
 def scan_from_zero(values, b_proj, c_proj, steps_dt, log_decay):
     row_count, head_count = steps_dt.shape
-    blocks = row_count // SPAN
-    causal = (jnp.arange(SPAN)[:, None] >= jnp.arange(SPAN)[None, :])[None]
+    causal = (jnp.arange(row_count)[:, None] >= jnp.arange(row_count)[None, :])[None]
 
     def one_block(carried, block_data):
         block_vals, b_blk, c_blk, dt_blk, la_blk = block_data
@@ -69,27 +73,16 @@
         scores = jnp.dot(c_blk, b_blk.T, precision=highest)
         scaled = block_vals * dt_blk[:, :, None]
         y_diag = jnp.einsum("htu,uhp->thp", weights * scores[None], scaled, precision=highest)
-        y_off = (
-            jnp.einsum("tn,hpn->thp", c_blk, carried, precision=highest)
-            * jnp.exp(cumulative)[:, :, None]
-        )
         ending = cumulative[-1]
         tail_decay = jnp.exp(ending[None, :] - cumulative)
-        updated = carried * jnp.exp(ending)[:, None, None] + jnp.einsum(
+        updated = jnp.einsum(
             "uhp,un->hpn", scaled * tail_decay[:, :, None], b_blk, precision=highest
         )
-        return (updated, y_diag + y_off)
-
-    stacked = (
-        values.reshape(blocks, SPAN, head_count, HEAD_DIM),
-        b_proj.reshape(blocks, SPAN, STATE),
-        c_proj.reshape(blocks, SPAN, STATE),
-        steps_dt.reshape(blocks, SPAN, head_count),
-        log_decay.reshape(blocks, SPAN, head_count),
-    )
+        return (updated, y_diag)
+
     initial = jnp.zeros((head_count, HEAD_DIM, STATE), jnp.float32)
-    last_state, outputs = lax.scan(one_block, initial, stacked)
-    return (outputs.reshape(row_count, head_count, HEAD_DIM), last_state)
+    last_state, outputs = one_block(initial, (values, b_proj, c_proj, steps_dt, log_decay))
+    return (outputs, last_state)
 
 
 def carry_term(c_proj, log_decay, entering):
@@ -98,10 +91,6 @@
         jnp.einsum("tn,hpn->thp", c_proj, entering, precision=highest)
         * jnp.exp(cumulative)[:, :, None]
     )
-
-
-def link_states(earlier, later):
-    return (earlier[0] * later[0], later[0][:, None, None] * earlier[1] + later[1])
 
 
 def token_sums(partial_sums):
@@ -137,12 +126,10 @@
     head_count = w_dt.shape[2]
     hidden = h_in
     kept = []
+    all_gain = lax.all_gather(norm_gain, "head", axis=1, tiled=True)
     for layer_idx in range(LAYERS):
-        gain_one = norm_gain[layer_idx]
-        full_hidden, full_gain = (
-            lax.all_gather(hidden, "head", axis=1, tiled=True),
-            lax.all_gather(gain_one, "head", axis=0, tiled=True),
-        )
+        full_hidden = lax.all_gather(hidden, "head", axis=1, tiled=True)
+        full_gain = all_gain[layer_idx]
         factor = lax.rsqrt(jnp.mean(full_hidden * full_hidden, axis=1) + epsilon)
         normed = (full_hidden * factor[:, None] * full_gain[None, :]).astype(jnp.bfloat16)
         gate_in = jnp.dot(normed, w_z[layer_idx], preferred_element_type=jnp.float32)
@@ -168,9 +155,9 @@
             scan_from_zero, values, b_proj, c_proj, steps_dt, log_decay
         )
         scanned, leaving = local_part
-        decays = jnp.exp(jnp.sum(log_decay, axis=0))
-        identity = (jnp.ones_like(decays), jnp.zeros_like(leaving))
-        entering = entering_2((decays, leaving), "seq", link_states, identity, False)[1]
+        log_total = jnp.sum(log_decay, axis=0)
+        decays = jnp.exp(log_total)
+        entering = entering_state(log_total, leaving, "seq", False)
         carried_part, carry_back = jax.vjp(carry_term, c_proj, log_decay, entering)
         mixed = scanned + carried_part + skip[layer_idx][None, :, None] * values
         gate_act = jax.nn.silu(gate_in)
@@ -194,6 +181,7 @@
                 mixed,
                 values,
                 decays,
+                log_total,
                 entering,
                 input_back,
                 block_back,
@@ -216,6 +204,7 @@
             mixed,
             values,
             decays,
+            log_total,
             entering,
             input_back,
             block_back,
@@ -238,8 +227,7 @@
         d_mixed = (d_gated * gate_act).reshape(row_count, head_count, HEAD_DIM)
         d_skipped = jnp.sum(d_mixed * values, axis=(0, 2))
         d_c_carry, d_la_carry, d_entering = carry_back(d_mixed)
-        back_identity = (jnp.ones_like(decays), jnp.zeros_like(d_entering))
-        leaving_grad = entering_2((decays, d_entering), "seq", link_states, back_identity, True)[1]
+        leaving_grad = entering_state(log_total, d_entering, "seq", True)
         d_decays = jnp.sum(leaving_grad * entering, axis=(1, 2)) * decays
         d_values, d_b_proj, d_c_local, d_steps, d_la_local = block_back((d_mixed, leaving_grad))
         d_values = d_values + skip[layer_idx][None, :, None] * d_mixed
@@ -291,61 +279,53 @@
         d_unit = d_normed * norm_gain[layer_idx][None, :]
         along_in = token_sums(jnp.sum(d_unit * centered, axis=1)) / D
         grad = grad + factor[:, None] * (d_unit - centered * along_in[:, None])
-        collected[layer_idx] = (
-            d_wz,
-            d_wx,
-            d_wdt,
-            d_cols,
+        weight_sums = (d_wz, d_wx, d_wdt, d_cols, d_wbc)
+        maps = jnp.concatenate([d_cweight[:, inner:].reshape(-1), d_cbias[inner:]])
+        vectors = (
             d_ngain,
-            d_cweight[:, :inner],
+            d_cweight[:, :inner].reshape(-1),
             d_cbias[:inner],
             d_ggain,
             d_dtbias,
             d_alog,
             d_skipped,
-            d_wbc,
-            d_cweight[:, inner:],
-            d_cbias[inner:],
-        )
-    stacks = [
-        jnp.stack([collected[layer_idx][member] for layer_idx in range(LAYERS)])
-        for member in range(14)
+        )
+        collected[layer_idx] = (weight_sums, vectors, maps)
+    sizes = [piece.shape[0] for piece in collected[0][1]]
+    maps = lax.psum(jnp.concatenate([entry[2] for entry in collected]), "head")
+    own = jnp.concatenate([piece for entry in collected for piece in entry[1]])
+    flat = lax.psum(jnp.concatenate([own, maps]), "seq")
+    maps = flat[own.shape[0] :].reshape(LAYERS, CONV + 1, -1)
+    flat = flat[: own.shape[0]].reshape(LAYERS, -1)
+    spots = [sum(sizes[:place]) for place in range(len(sizes) + 1)]
+    ngain, cw, cb, ggain, dtb, alog, skipped = [
+        flat[:, spots[place] : spots[place + 1]] for place in range(len(sizes))
     ]
-    weight_sums = (
-        lax.psum_scatter(
-            stacks[0].astype(jnp.bfloat16), "seq", scatter_dimension=1, tiled=True
-        ).astype(jnp.float32),
-        lax.psum_scatter(
-            stacks[1].astype(jnp.bfloat16), "seq", scatter_dimension=1, tiled=True
-        ).astype(jnp.float32),
-        lax.psum_scatter(
-            stacks[2].astype(jnp.bfloat16), "seq", scatter_dimension=1, tiled=True
-        ).astype(jnp.float32),
-        lax.psum_scatter(
-            stacks[3].astype(jnp.bfloat16), "seq", scatter_dimension=2, tiled=True
-        ).astype(jnp.float32),
-    )
-    vector_sums = lax.psum(
-        (stacks[4], stacks[5], stacks[6], stacks[7], stacks[8], stacks[9], stacks[10]), "seq"
-    )
-    shared_sums = lax.psum((stacks[11], stacks[12], stacks[13]), ("seq", "head"))
+
+    def layers(member, dimension):
+        stack = jnp.stack([entry[0][member] for entry in collected]).astype(jnp.bfloat16)
+        return lax.psum_scatter(stack, "seq", scatter_dimension=dimension, tiled=True)
+
+    shared = lax.psum(layers(4, 1).astype(jnp.float32), "head")
+    shared = lax.all_gather(shared.astype(jnp.bfloat16), "seq", axis=1, tiled=True)
+
     return (
         hidden,
         grad,
-        vector_sums[0],
-        weight_sums[0],
-        weight_sums[1],
-        shared_sums[0],
-        weight_sums[2],
-        vector_sums[1],
-        vector_sums[2],
-        shared_sums[1],
-        shared_sums[2],
-        vector_sums[4],
-        vector_sums[5],
-        vector_sums[6],
-        vector_sums[3],
-        weight_sums[3],
+        ngain,
+        layers(0, 1).astype(jnp.float32),
+        layers(1, 1).astype(jnp.float32),
+        shared.astype(jnp.float32),
+        layers(2, 1).astype(jnp.float32),
+        cw.reshape(LAYERS, CONV, inner),
+        cb,
+        maps[:, :CONV],
+        maps[:, CONV],
+        dtb,
+        alog,
+        skipped,
+        ggain,
+        layers(3, 2).astype(jnp.float32),
     )
 
 

time: 1010 us -> 1010 us (level)
  waiting for transfers between devices: 475 us -> 574 us
  blocking collectives: 185 us -> 100 us
  local copies, waits for them, and re-layouts: 96.9 us -> 117 us
  other arithmetic: 110 us -> 90.9 us
  matrix products: 100 us -> 86.4 us
    psum x1, waiting for transfers between devices: 137 us -> 13.8 us  [local(): shared = lax.psum(layers(4, 1).astype(jnp.float32), 'head')]
    unnamed x17 -> x19, waiting for transfers between devices: 32.7 us -> 133 us
    reduce_scatter x2 -> x3, waiting for transfers between devices: 95.3 us -> 179 us  [layers(): lax.psum_scatter(stack, 'seq', scatter_dimension=dimension, tiled=True)]
    unnamed x2 -> x0, blocking collectives: 43.9 us -> none
    all_gather x6 -> x7, waiting for transfers between devices: 112 us -> 155 us  [the longest x4 132 us: entering_state(): pieces = lax.all_gather(packed, axis)]
    psum x2 -> x1, blocking collectives: 80 us -> 38.1 us  [local(): flat = lax.psum(jnp.concatenate([own, maps]), 'seq')]
    select_n x28 -> x4, other arithmetic: 29.4 us -> 2.98 us  [entering_state(): weights = jnp.where(used[:, None], jnp.exp(total), 0.0)]
    mul x34 -> x84, local copies, waits for them, and re-layouts: 31.6 us -> 56.1 us  [the longest x56 27.9 us: entering_state(): result = result + weights[place][:, None, None] * values[place]]
  transfers between devices with their start and end apart: 19 -> 21, of which waited for: 17 -> 20; matrix products, arithmetic and copies ran while one was open for 13% -> 13% of each run, Pallas kernels for 0% -> 0%
where the time goes in v1:
time: 1010 us; the launch traced here: 996 us
  waiting for transfers between devices  574 us (57%)
  local copies, waits for them, and re-layouts  117 us (12%)
  blocking collectives  100 us (10%)
  other arithmetic  90.9 us (9%)
  matrix products  86.4 us (9%)
  between operations  16.9 us (2%)
  starting transfers between devices  10.2 us (1%)
    reduce_scatter x3, waiting for transfers between devices, layers(): lax.psum_scatter(stack, 'seq', scatter_dimension=dimension, tiled=True)  179 us
    unnamed x19, waiting for transfers between devices  133 us
    all_gather x4, waiting for transfers between devices, entering_state(): pieces = lax.all_gather(packed, axis)  132 us
    reduce_scatter x2, waiting for transfers between devices, local(): lax.psum_scatter(contract_first(out_weight, scaled.T), 'head', scatter_di...  43.5 us
    psum x6, blocking collectives, token_sums(): return lax.psum(partial_sums, 'head')  42 us
    reduce_scatter x2, waiting for transfers between devices, local(): lax.psum_scatter(product(wz_now, d_gate_b) + product(wx_now, d_x_b) + pro...  39.4 us
    psum x1, blocking collectives, local(): flat = lax.psum(jnp.concatenate([own, maps]), 'seq')  38.1 us
    mul x56, local copies, waits for them, and re-layouts, entering_state(): result = result + weights[place][:, None, None] * values[place]  27.9 us
  transfers between devices with their start and end apart: 21, of which 20 were waited for; matrix products, arithmetic and copies ran while one was open for 13% of the time, Pallas kernels for 0%

profile of v1, /device:TPU:0, one launch (start us, length us, event | category | flops | bytes accessed | tf_op | source)
XLA Modules:
  0.0 995.7 jit_solution(15239382014503866556)
XLA Ops:
  9.3 6.3 all_gather.43
  21.7 7.4 all-gather.12.cloned.1.call-done
  35.5 3.4 collective-permute-start
  47.7 46.2 %all-gather.18.cloned.1.call-done = f32[4160,128]{1,0:T(8,128)} async-done(((f32[520,128]{1,0:T(8,128)}), f32[4160,128]{1,0:T(8,128)}) %all-gather.18.cloned.1.call-update) | async-done | bytes 2129936 | tf_op jit(solution)/shard_map/all_gather | solution.py:30
  94.7 2.6 fusion.338
  101.0 2.5 fusion.53
  104.6 2.5 multiply_reduce_fusion.25
  107.2 5.8 psum.63
  113.0 2.7 convolution_bitcast_fusion.1
  115.8 23.7 %reduce-scatter.14.cloned.1.call-done = f32[256,256]{0,1:T(8,128)} async-done(((f32[1024,256]{0,1:T(8,128)}), f32[256,256]{0,1:T(8,128)}) %reduce-scatter.14.cloned.1.call-update) | async-done | bytes 262160 | tf_op jit(solution)/shard_map/reduce_scatter | solution.py:168
  142.5 15.7 %all-gather.14.cloned.1.call-done = f32[256,1024]{1,0:T(8,128)} async-done(((f32[256,256]{1,0:T(8,128)}), f32[256,1024]{1,0:T(8,128)}) %all-gather.14.cloned.1.call-update) | async-done | bytes 1048592 | tf_op jit(solution)/shard_map/all_gather | solution.py:131
  164.1 3.4 collective-permute-start.1
  170.1 2.4 fusion.114
  180.9 7.4 all_gather.49
  196.8 33.4 %all-gather.20.cloned.1.call-done = f32[4160,128]{1,0:T(8,128)} async-done(((f32[520,128]{1,0:T(8,128)}), f32[4160,128]{1,0:T(8,128)}) %all-gather.20.cloned.1.call-update) | async-done | bytes 2129936 | tf_op jit(solution)/shard_map/all_gather | solution.py:30
  231.0 2.9 fusion.337
  236.7 2.2 fusion.170
  239.1 3.3 fusion.44
  244.4 2.8 multiply_reduce_fusion.24
  247.2 6.2 psum.64
  254.1 3.4 multiply_reduce_fusion.13
  257.5 7.3 psum.65
  265.4 4.0 multiply_reduce_fusion.12
  295.5 2.8 fusion.61
  298.4 3.9 fusion.35
  302.3 20.7 %all-gather.22.cloned.1.call-done = f32[4160,128]{1,0:T(8,128)} async-done(((f32[520,128]{1,0:T(8,128)}), f32[4160,128]{1,0:T(8,128)}) %all-gather.22.cloned.1.call-update) | async-done | bytes 2129936 | tf_op jit(solution)/shard_map/all_gather | solution.py:30
  323.7 2.9 fusion.336
  339.7 2.3 fusion.153
  342.1 3.5 multiply_reduce_fusion.20
  345.6 2.6 reduce-window.46
  351.8 3.8 multiply_reduce_fusion.29
  357.2 2.5 reduce-window.50
  359.8 2.2 convolution_bitcast_fusion.5
  371.1 3.2 collective-permute-done.2
  377.6 2.9 convolution_bitcast_fusion
  386.9 15.0 %reduce-scatter.18.cloned.1.call-done = f32[256,256]{0,1:T(8,128)} async-done(((f32[1024,256]{0,1:T(8,128)}), f32[256,256]{0,1:T(8,128)}) %reduce-scatter.18.cloned.1.call-update) | async-done | bytes 262160 | tf_op jit(solution)/shard_map/reduce_scatter | solution.py:268
  403.7 5.7 psum.66
  409.4 19.8 %reduce-scatter.16.cloned.1.call-done = f32[256,256]{0,1:T(8,128)} async-done(((f32[1024,256]{0,1:T(8,128)}), f32[256,256]{0,1:T(8,128)}) %reduce-scatter.16.cloned.1.call-update) | async-done | bytes 262160 | tf_op jit(solution)/shard_map/reduce_scatter | solution.py:168
  429.3 2.1 fusion.330
  431.4 6.6 all_gather.52
  438.0 3.3 multiply_reduce_fusion.15
  441.3 6.9 psum.67
  448.2 3.9 multiply_reduce_fusion.14
  469.7 4.9 fusion.37
  474.6 32.1 %all-gather.24.cloned.1.call-done = f32[4160,128]{1,0:T(8,128)} async-done(((f32[520,128]{1,0:T(8,128)}), f32[4160,128]{1,0:T(8,128)}) %all-gather.24.cloned.1.call-update) | async-done | bytes 2129936 | tf_op jit(solution)/shard_map/all_gather | solution.py:30
  507.4 2.8 fusion.335
  517.7 2.3 fusion.136
  520.1 4.2 multiply_reduce_fusion.16
  525.6 3.8 multiply_reduce_fusion.27
  535.0 4.0 collective-permute-done.3
  545.4 2.5 reduce-window.54
  548.6 2.5 reduce-window.56
  551.6 54.1 %reduce-scatter.26.cloned.1.call-done = bf16[2,128,256]{2,1,0:T(8,128)(2,1)} async-done(((bf16[2,1024,256]{2,1,0:T(8,128)(2,1)}), bf16[2,128,256]{2,1,0:T(8,128)(2,1)}) %reduce-scatter.26.cloned.1.call-update) | async-done | bytes 131088 | tf_op jit(solution)/shard_map/reduce_scatter | solution.py:307
  609.0 4.0 copy.195
  613.0 3.5 copy.206
  625.1 13.8 %all-reduce.29.cloned.1.call-done = bf16[2,128,256]{2,1,0:T(8,128)(2,1)} async-done(((bf16[2,128,256]{2,1,0:T(8,128)(2,1)}), bf16[2,128,256]{2,1,0:T(8,128)(2,1)}) %all-reduce.29.cloned.1.call-update) | async-done | bytes 131088 | tf_op jit(solution)/shard_map/psum | solution.py:309
  642.9 61.9 %reduce-scatter.28.cloned.1.call-done = bf16[128,16]{1,0:T(8,128)(2,1)} async-done(((bf16[1024,16]{1,0:T(8,128)(2,1)}), bf16[128,16]{1,0:T(8,128)(2,1)}) %reduce-scatter.28.cloned.1.call-update) | async-done | bytes 4112
  706.3 70.1 %reduce-scatter.30.cloned.1.call-done = bf16[128,1024]{1,0:T(8,128)(2,1)} async-done(((bf16[1024,1024]{1,0:T(8,128)(2,1)}), bf16[128,1024]{1,0:T(8,128)(2,1)}) %reduce-scatter.30.cloned.1.call-update) | async-done | bytes 262160
  778.5 69.2 %reduce-scatter.22.cloned.1.call-done = bf16[2,128,512]{2,1,0:T(8,128)(2,1)} async-done(((bf16[2,1024,512]{2,1,0:T(8,128)(2,1)}), bf16[2,128,512]{2,1,0:T(8,128)(2,1)}) %reduce-scatter.22.cloned.1.call-update) | async-done | bytes 262160 | tf_op jit(solution)/shard_map/reduce_scatter | solution.py:307
  849.6 24.4 %reduce-scatter.20.cloned.1.call-done = f32[256,256]{0,1:T(8,128)} async-done(((f32[1024,256]{0,1:T(8,128)}), f32[256,256]{0,1:T(8,128)}) %reduce-scatter.20.cloned.1.call-update) | async-done | bytes 262160 | tf_op jit(solution)/shard_map/reduce_scatter | solution.py:268
  875.1 10.1 %all-reduce.26 = (f32[256]{0:T(256)S(1)}, f32[2560]{0:T(1024)S(1)}) all-reduce(f32[256]{0:T(256)S(1)} %get-tuple-element.63, f32[2560]{0:T(1024)S(1)} %pad_maximum_fusion.11), channel_id=1, replica_groups=mesh['seq'=8,'head'=4] {'head'}, use_global_device_ids=true, to_apply=%region_53.55 | all-reduce | flops 2816 | bytes 22528 | tf_op jit(solution)/shard_map/psum | solution.py:97
  885.4 38.1 %psum.70 = f32[9264]{0:T(1024)S(1)} all-reduce(f32[9264]{0:T(1024)S(1)} %concatenate.55), channel_id=1, replica_groups=mesh['seq'=8,'head'=4] {'seq'}, use_global_device_ids=true, to_apply=%region_77.79 | all-reduce | flops 9264 | bytes 74112 | tf_op jit(solution)/shard_map/psum | solution.py:297
  929.1 2.7 convert_element_type.79
  931.8 55.3 %reduce-scatter.24.cloned.1.call-done = bf16[2,128,512]{2,1,0:T(8,128)(2,1)} async-done(((bf16[2,1024,512]{2,1,0:T(8,128)(2,1)}), bf16[2,128,512]{2,1,0:T(8,128)(2,1)}) %reduce-scatter.24.cloned.1.call-update) | async-done | bytes 262160 | tf_op jit(solution)/shard_map/reduce_scatter | solution.py:307
  (728 shorter events, 198.2 us)
Async XLA Ops:
  7.2 24.6 %copy-start.58 = (bf16[2,1024,8]{1,2,0:T(8,128)(2,1)S(1)}, bf16[2,1024,8]{1,2,0:T(8,128)(2,1)}, u32[]{:S(2)}) copy-start(bf16[2,1024,8]{1,2,0:T(8,128)(2,1)} %param.22) | copy-start | bytes 98308
  7.2 26.1 %copy-start.20 = (bf16[2,1024,256]{2,1,0:T(8,128)(2,1)S(1)}, bf16[2,1024,256]{2,1,0:T(8,128)(2,1)}, u32[]{:S(2)}) copy-start(bf16[2,1024,256]{2,1,0:T(8,128)(2,1)} %param.21) | copy-start | bytes 3145732
  7.2 21.8 %all-gather.12.cloned.1.call-start = ((), (), s32[]{:S(2)}) async-start(), calls=%async_computation.9 | async-start | bytes 1310720 | tf_op jit(solution)/shard_map/all_gather | solution.py:131
  7.9 86.0 %all-gather.18.cloned.1.call-start = ((), (), s32[]{:S(2)}) async-start(), calls=%async_computation.20 | async-start | bytes 2396160 | tf_op jit(solution)/shard_map/all_gather | solution.py:30
  16.4 23.9 %copy-start.80 = (f32[768]{0:T(1024)}, f32[768]{0:T(1024)S(1)}, u32[]{:S(2)}) copy-start(f32[768]{0:T(1024)S(1)} %get-tuple-element.72) | copy-start | bytes 9220
  16.4 23.9 %copy-start.82 = (f32[768]{0:T(1024)}, f32[768]{0:T(1024)S(1)}, u32[]{:S(2)}) copy-start(f32[768]{0:T(1024)S(1)} %get-tuple-element.73) | copy-start | bytes 9220
  16.4 23.9 %copy-start.84 = (f32[768]{0:T(1024)}, f32[768]{0:T(1024)S(1)}, u32[]{:S(2)}) copy-start(f32[768]{0:T(1024)S(1)} %get-tuple-element.74) | copy-start | bytes 9220
  16.4 23.9 %copy-start.86 = (f32[768]{0:T(1024)}, f32[768]{0:T(1024)S(1)}, u32[]{:S(2)}) copy-start(f32[768]{0:T(1024)S(1)} %get-tuple-element.75) | copy-start | bytes 9220
  21.7 12.0 %copy-start.139 = (f32[8]{0:T(128)}, f32[8]{0:T(128)S(1)}, u32[]{:S(2)}) copy-start(f32[8]{0:T(128)S(1)} %get-tuple-element.223) | copy-start | bytes 100
  35.5 4.8 collective-permute-start
  42.0 59.0 %copy-start.37 = (f32[256,512]{0,1:T(8,128)}, f32[256,512]{0,1:T(8,128)S(1)}, u32[]{:S(2)}) copy-start(f32[256,512]{0,1:T(8,128)S(1)} %copy.164) | copy-start | bytes 1572868
  43.5 96.0 %reduce-scatter.14.cloned.1.call-start = ((), (), s32[]{:S(2)}) async-start(), calls=%async_computation.10 | async-start | bytes 1310720 | tf_op jit(solution)/shard_map/reduce_scatter | solution.py:168
  46.5 66.4 %copy-start.97 = (f32[1,512]{1,0:T(1,128)}, f32[1,512]{1,0:T(1,128)S(1)}, u32[]{:S(2)}) copy-start(f32[1,512]{1,0:T(1,128)S(1)} %get-tuple-element.193) | copy-start | bytes 6148
  46.6 54.4 %copy-start.93 = (f32[8,256]{1,0:T(8,128)}, f32[8,256]{1,0:T(8,128)S(1)}, u32[]{:S(2)}) copy-start(f32[8,256]{1,0:T(8,128)S(1)} %add_bitcast_fusion.3) | copy-start | bytes 24580
  107.2 34.0 %copy-start.13 = (f32[256,512]{1,0:T(8,128)}, f32[256,512]{1,0:T(8,128)S(1)}, u32[]{:S(2)}) copy-start(f32[256,512]{1,0:T(8,128)S(1)} %get-tuple-element.103) | copy-start | bytes 1572868
  107.2 32.3 %copy-start.18 = (f32[256,256]{1,0:T(8,128)S(1)}, f32[256,256]{1,0:T(8,128)}, u32[]{:S(2)}) copy-start(f32[256,256]{1,0:T(8,128)} %param.17) | copy-start | bytes 786436
  113.0 28.2 %copy-start.113 = (f32[256]{0:T(256)}, f32[256]{0:T(256)S(1)}, u32[]{:S(2)}) copy-start(f32[256]{0:T(256)S(1)} %add_rsqrt_fusion.2) | copy-start | bytes 3076
  113.0 28.3 %copy-start.108 = (f32[4,256]{1,0:T(4,128)S(1)}, f32[4,256]{1,0:T(4,128)}, u32[]{:S(2)}) copy-start(f32[4,256]{1,0:T(4,128)} %get-tuple-element.171) | copy-start | bytes 12292
  113.0 28.9 %copy-start.136 = (f32[1,512]{1,0:T(1,128)S(1)}, f32[1,512]{1,0:T(1,128)}, u32[]{:S(2)}) copy-start(f32[1,512]{1,0:T(1,128)} %get-tuple-element.202) | copy-start | bytes 6148
  113.0 28.9 %copy-start.171 = (f32[1,256]{1,0:T(1,128)S(1)}, f32[1,256]{1,0:T(1,128)}, u32[]{:S(2)}) copy-start(f32[1,256]{1,0:T(1,128)} %get-tuple-element.214) | copy-start | bytes 3076
  115.7 42.5 %all-gather.14.cloned.1.call-start = ((), (), s32[]{:S(2)}) async-start(), calls=%async_computation.11 | async-start | bytes 1310720 | tf_op jit(solution)/shard_map/all_gather | solution.py:131
  141.2 89.0 %all-gather.20.cloned.1.call-start = ((), (), s32[]{:S(2)}) async-start(), calls=%async_computation.21 | async-start | bytes 2396160 | tf_op jit(solution)/shard_map/all_gather | solution.py:30
  141.9 28.2 %copy-start.88 = (f32[768]{0:T(1024)}, f32[768]{0:T(1024)S(1)}, u32[]{:S(2)}) copy-start(f32[768]{0:T(1024)S(1)} %get-tuple-element.68) | copy-start | bytes 9220
  162.4 28.8 %copy-start.59 = (f32[256,8]{0,1:T(8,128)}, f32[256,8]{0,1:T(8,128)S(1)}, u32[]{:S(2)}) copy-start(f32[256,8]{0,1:T(8,128)S(1)} %get-tuple-element.170) | copy-start | bytes 24580
  164.1 4.8 collective-permute-start.1
  167.6 20.7 %copy-start.65 = (f32[256,8]{0,1:T(8,128)}, f32[256,8]{0,1:T(8,128)S(1)}, u32[]{:S(2)}) copy-start(f32[256,8]{0,1:T(8,128)S(1)} %subtract_exponential_fusion) | copy-start | bytes 24580
  167.6 11.3 %copy-start.78 = (f32[520]{0:T(1024)}, f32[520]{0:T(1024)S(1)}, u32[]{:S(2)}) copy-start(f32[520]{0:T(1024)S(1)} %pad.124.clone) | copy-start | bytes 6244
  179.8 14.3 %copy-start.121 = (f32[8,2]{0,1:T(2,128)S(1)}, f32[8,2]{0,1:T(2,128)}, u32[]{:S(2)}) copy-start(f32[8,2]{0,1:T(2,128)} %copy-done.120) | copy-start | bytes 196
  179.8 143.1 %all-gather.22.cloned.1.call-start = ((), (), s32[]{:S(2)}) async-start(), calls=%async_computation.22 | async-start | bytes 2396160 | tf_op jit(solution)/shard_map/all_gather | solution.py:30
  244.4 9.7 copy-start.100
  254.1 15.3 %copy-start.116 = (f32[256]{0:T(256)}, f32[256]{0:T(256)S(1)}, u32[]{:S(2)}) copy-start(f32[256]{0:T(256)S(1)} %add_rsqrt_fusion) | copy-start | bytes 3076
  274.9 127.0 %reduce-scatter.18.cloned.1.call-start = ((), (), s32[]{:S(2)}) async-start(), calls=%async_computation.13 | async-start | bytes 1310720 | tf_op jit(solution)/shard_map/reduce_scatter | solution.py:268
  327.3 14.8 %copy-start.61 = (f32[256,8]{0,1:T(8,128)S(1)}, f32[256,8]{0,1:T(8,128)}, u32[]{:S(2)}) copy-start(f32[256,8]{0,1:T(8,128)} %copy-done.59) | copy-start | bytes 24580
  327.3 14.8 %copy-start.66 = (f32[256,8]{0,1:T(8,128)S(1)}, f32[256,8]{0,1:T(8,128)}, u32[]{:S(2)}) copy-start(f32[256,8]{0,1:T(8,128)} %copy-done.65) | copy-start | bytes 24580
  327.3 14.8 %copy-start.96 = (f32[8,256]{1,0:T(8,128)S(1)}, f32[8,256]{1,0:T(8,128)}, u32[]{:S(2)}) copy-start(f32[8,256]{1,0:T(8,128)} %add_bitcast_fusion.1) | copy-start | bytes 24580
  368.7 5.6 collective-permute-start.2
  374.4 89.4 %copy-start.5 = (f32[256,768]{1,0:T(8,128)}, f32[256,768]{1,0:T(8,128)S(1)}, u32[]{:S(2)}) copy-start(f32[256,768]{1,0:T(8,128)S(1)} %slice_add_fusion.1) | copy-start | bytes 2359300
  377.5 51.7 %reduce-scatter.16.cloned.1.call-start = ((), (), s32[]{:S(2)}) async-start(), calls=%async_computation.12 | async-start | bytes 1310720 | tf_op jit(solution)/shard_map/reduce_scatter | solution.py:168
  380.5 21.4 %copy-start.112 = (f32[256]{0:T(256)S(1)}, f32[256]{0:T(256)}, u32[]{:S(2)}) copy-start(f32[256]{0:T(256)} %copy-done.111) | copy-start | bytes 3076
  380.5 126.2 %all-gather.24.cloned.1.call-start = ((), (), s32[]{:S(2)}) async-start(), calls=%async_computation.23 | async-start | bytes 2396160 | tf_op jit(solution)/shard_map/all_gather | solution.py:30
  384.9 53.1 %copy-start.98 = (f32[1,512]{1,0:T(1,128)S(1)}, f32[1,512]{1,0:T(1,128)}, u32[]{:S(2)}) copy-start(f32[1,512]{1,0:T(1,128)} %copy-done.97) | copy-start | bytes 6148
  384.9 53.1 %copy-start.114 = (f32[256]{0:T(256)S(1)}, f32[256]{0:T(256)}, u32[]{:S(2)}) copy-start(f32[256]{0:T(256)} %copy-done.113) | copy-start | bytes 3076
  456.7 149.1 %reduce-scatter.26.cloned.1.call-start = ((), (), s32[]{:S(2)}) async-start(), calls=%async_computation.17 | async-start | bytes 1179648 | tf_op jit(solution)/shard_map/reduce_scatter | solution.py:307
  510.3 9.7 copy-start.38
  533.5 5.6 collective-permute-start.3
  541.9 9.3 copy-start.175
  541.9 9.3 copy-start.68
  541.9 9.3 copy-start.132
  541.9 96.9 %all-reduce.29.cloned.1.call-start = ((), (), s32[]{:S(2)}) async-start(), calls=%async_computation.18 | async-start | bytes 262144 | tf_op jit(solution)/shard_map/psum | solution.py:309
  605.8 99.0 %reduce-scatter.28.cloned.1.call-start = ((), (), s32[]{:S(2)}) async-start(), calls=%async_computation.24 | async-start | bytes 294912
  607.2 169.1 %reduce-scatter.30.cloned.1.call-start = ((), (), s32[]{:S(2)}) async-start(), calls=%async_computation.25 | async-start | bytes 2359296
  616.6 231.2 %reduce-scatter.22.cloned.1.call-start = ((), (), s32[]{:S(2)}) async-start(), calls=%async_computation.15 | async-start | bytes 2359296 | tf_op jit(solution)/shard_map/reduce_scatter | solution.py:307
  620.0 254.0 %reduce-scatter.20.cloned.1.call-start = ((), (), s32[]{:S(2)}) async-start(), calls=%async_computation.14 | async-start | bytes 1310720 | tf_op jit(solution)/shard_map/reduce_scatter | solution.py:268
  623.4 15.6 %copy-start.6 = (f32[256,768]{1,0:T(8,128)S(1)}, f32[256,768]{1,0:T(8,128)}, u32[]{:S(2)}) copy-start(f32[256,768]{1,0:T(8,128)} %copy-done.5) | copy-start | bytes 2359300
  625.0 304.1 %all-gather.16.cloned.1.call-start = ((), (), s32[]{:S(2)}) async-start(), calls=%async_computation.19 | async-start | bytes 1179648 | tf_op jit(solution)/shard_map/all_gather | solution.py:310
  638.9 348.2 %reduce-scatter.24.cloned.1.call-start = ((), (), s32[]{:S(2)}) async-start(), calls=%async_computation.16 | async-start | bytes 2359296 | tf_op jit(solution)/shard_map/reduce_scatter | solution.py:307
  641.5 232.5 %copy-start.19 = (f32[256,256]{1,0:T(8,128)S(1)}, f32[256,256]{1,0:T(8,128)}, u32[]{:S(2)}) copy-start(f32[256,256]{1,0:T(8,128)} %param.17) | copy-start | bytes 786436
  641.5 232.5 %copy-start.110 = (f32[256]{0:T(256)S(1)}, f32[256]{0:T(256)}, u32[]{:S(2)}) copy-start(f32[256]{0:T(256)} %copy-done.109) | copy-start | bytes 3076
  641.5 232.5 %copy-start.119 = (f32[1,256]{1,0:T(1,128)S(1)}, f32[1,256]{1,0:T(1,128)}, u32[]{:S(2)}) copy-start(f32[1,256]{1,0:T(1,128)} %get-tuple-element.212) | copy-start | bytes 3076
  641.5 243.8 %copy-start.167 = (f32[256]{0:T(256)S(1)}, f32[256]{0:T(256)}, u32[]{:S(2)}) copy-start(f32[256]{0:T(256)} %get-tuple-element.60) | copy-start | bytes 3076
  641.5 243.8 %copy-start.180 = (f32[512]{0:T(512)S(1)}, f32[512]{0:T(512)}, u32[]{:S(2)}) copy-start(f32[512]{0:T(512)} %get-tuple-element.52) | copy-start | bytes 6148
  641.5 243.8 %copy-start.181 = (f32[512]{0:T(512)S(1)}, f32[512]{0:T(512)}, u32[]{:S(2)}) copy-start(f32[512]{0:T(512)} %get-tuple-element.54) | copy-start | bytes 6148
  641.6 243.8 %copy-start.182 = (f32[8]{0:T(128)S(1)}, f32[8]{0:T(128)}, u32[]{:S(2)}) copy-start(f32[8]{0:T(128)} %get-tuple-element.80) | copy-start | bytes 100
  641.6 285.8 %copy-start.47 = (f32[256,256]{1,0:T(8,128)S(1)}, f32[256,256]{1,0:T(8,128)}, u32[]{:S(2)}) copy-start(f32[256,256]{1,0:T(8,128)} %get-tuple-element.92) | copy-start | bytes 786436
  (145 other events, 497.7 us)
Sparse Core Ops, SparseCore 0:
  9.6 19.4 all-gather.11
  43.6 50.2 all-gather.17
  115.9 23.5 reduce-scatter.13
  141.5 16.6 all-gather.13
  179.9 50.2 all-gather.19
  275.0 47.8 all-gather.21
  377.6 24.2 reduce-scatter.17
  404.4 24.7 reduce-scatter.15
  456.8 49.8 all-gather.23
  542.0 63.7 reduce-scatter.25
  608.1 30.7 all-reduce.28
  642.6 62.0 reduce-scatter.27
  708.3 68.0 reduce-scatter.29
  780.3 67.4 reduce-scatter.21
  850.1 23.8 reduce-scatter.19
  876.0 40.8 all-gather.15
  920.3 66.8 reduce-scatter.23
